TPU v7x, 32 devices: a whole 2x2x4 slice. The times are simulated.
32 devices in a mesh: rep: 2 (over x), node: 8 (over z, y), local: 2 (over core).
Axes of the slice: x: 2, y: 2, z: 4, core: 2. Of those that a mesh axis runs over, the one named last changes fastest.
Arguments:
- tokens: bfloat16 [2048, 7168], P(('rep', 'node', 'local')), parts along dimension 0, may hold values from -6 to 6
- gate_ids: int32 [2048, 4], P(('rep', 'node', 'local')), parts along dimension 0, may hold values from 0 to 7, all different within a row; in each aligned block of 64 rows (0 to 63, 64 to 127, ...) at most 64 rows name the same one
- gate_values: bfloat16 [2048, 4], P(('rep', 'node', 'local')), parts along dimension 0, may hold values from 0.049804688 to 1
- w_gate: bfloat16 [8, 7168, 1024], P('node', None, 'local'), may hold values from -0.0625 to 0.0625
- w_up: bfloat16 [8, 7168, 1024], P('node', None, 'local'), may hold values from -0.0625 to 0.0625
- w_down: bfloat16 [8, 1024, 7168], P('node', 'local'), may hold values from -0.1875 to 0.1875
Outputs:
- mixed: bfloat16 [2048, 7168], P(('rep', 'node', 'local')), parts along dimension 0
There are 2 independent parts, one for each index of `rep`. A program takes and returns all parts, laid end to end along the dimension named above; an argument that names none is the same for every part. Nothing has to cross between parts.
Inputs may be any that keep to these rules, and one draw needn't show every extreme that they name: `gate_ids`: each row names 4 different experts. Within the rows of one device, no expert is named by more than 64 rows, and in every draw some expert is named by exactly 64 rows of some device.
All inputs are finite; a program needn't handle non-finite values.
Results may differ from a plain program's by a relative error of at most 0.0065.
Values may be sent and summed in bfloat16 or wider, within the bound.
A program may use at most 128 MiB of HBM per device.

v0:
```python
import jax
import jax.numpy as jnp
from jax import lax
from jax.sharding import PartitionSpec as P


def per_device(tokens, gate_ids, gate_values, w_gate, w_up, w_down):
    node_count = lax.axis_size("node")
    token_count = tokens.shape[0]
    choose_count = gate_ids.shape[1]
    width = tokens.shape[1]
    capacity = 2 * token_count * choose_count // node_count
    flat_ids = gate_ids.reshape(-1)
    expert_row = jnp.arange(node_count, dtype=jnp.int32)
    onehot = (flat_ids[:, None] == expert_row[None, :]).astype(jnp.int32)
    earlier = jnp.cumsum(onehot, axis=0) - onehot
    within = jnp.sum(earlier * onehot, axis=1)
    slot = (flat_ids * capacity + within).reshape(token_count, choose_count)
    slot_row = jnp.arange(node_count * capacity, dtype=jnp.int32)
    matches = slot[:, :, None] == slot_row[None, None, :]
    select = jnp.any(matches, axis=1).astype(jnp.bfloat16)
    combine_table = jnp.sum(
        jnp.where(matches, gate_values.astype(jnp.float32)[:, :, None], jnp.float32(0.0)), axis=1
    ).astype(jnp.bfloat16)
    outgoing = jnp.einsum("ts,td->sd", select, tokens, preferred_element_type=jnp.float32).astype(
        jnp.bfloat16
    )
    outgoing = outgoing.reshape(node_count, capacity, width)
    gathered = lax.all_gather(
        lax.all_to_all(outgoing, "node", split_axis=0, concat_axis=0, tiled=True),
        "local",
        axis=0,
        tiled=True,
    )
    rows = gathered.reshape(-1, width)
    gate_act = jnp.dot(rows, w_gate[0], preferred_element_type=jnp.float32)
    up_act = jnp.dot(rows, w_up[0], preferred_element_type=jnp.float32)
    hidden = (jax.nn.silu(gate_act) * up_act).astype(jnp.bfloat16)
    partial_value = (
        jnp.dot(hidden, w_down[0], preferred_element_type=jnp.float32)
        .astype(jnp.bfloat16)
        .reshape(gathered.shape)
    )
    partial_value = lax.optimization_barrier(partial_value).astype(jnp.float32)
    own_rows = lax.psum_scatter(
        partial_value.astype(jnp.bfloat16), "local", scatter_dimension=0, tiled=True
    )
    expert_out = lax.all_to_all(own_rows, "node", split_axis=0, concat_axis=0, tiled=True)
    result = jnp.dot(
        combine_table,
        expert_out.reshape(node_count * capacity, width),
        preferred_element_type=jnp.float32,
    )
    return result.astype(jnp.bfloat16)


def solution(mesh):
    return jax.shard_map(
        per_device,
        mesh=mesh,
        in_specs=(
            P(("rep", "node", "local"), None),
            P(("rep", "node", "local"), None),
            P(("rep", "node", "local"), None),
            P("node", None, "local"),
            P("node", None, "local"),
            P("node", "local", None),
        ),
        out_specs=P(("rep", "node", "local"), None),
        check_vma=False,
    )
```

profile of v0, /device:TPU:0, one launch (start us, length us, event | category | flops | bytes accessed | tf_op | source)
XLA Modules:
  0.0 445.9 jit_solution(14984800012365417282)
XLA Ops:
  6.5 0.0 copy-start
  6.5 0.0 all-gather.2.cloned.1.call-start
  6.5 0.9 copy.24
  7.4 0.1 eq.42
  7.5 0.1 eq.38
  7.6 0.6 reduce-window.6
  8.2 0.2 slice_reduce_fusion
  8.5 0.1 fusion.10
  8.6 0.1 reduce_sum.21
  8.7 0.1 copy.26
  8.7 0.7 multiply_add_fusion
  9.4 0.1 fusion.7
  9.6 0.0 copy-done
  9.6 2.1 convolution_convert_fusion.1
  11.7 167.8 %all_to_all.10 = bf16[8,64,7168]{2,1,0:T(8,128)(2,1)} all-to-all(bf16[8,64,7168]{2,1,0:T(8,128)(2,1)S(1)} %bitcast.30), channel_id=1, replica_groups=mesh['rep'=2,'node'=8,'local'=2] {'node'}, dimensions={0} | all-to-all | bytes 14680064 | tf_op jit(solution)/shard_map/all_to_all | solution.py:30
  179.5 0.0 all-gather.2.cloned.1.call-update
  179.5 0.0 reduce-scatter.2.cloned.1.call-start
  179.6 26.1 %all-gather.2.cloned.1.call-done = bf16[16,64,7168]{2,1,0:T(8,128)(2,1)} async-done(((bf16[8,64,7168]{2,1,0:T(8,128)(2,1)}), bf16[16,64,7168]{2,1,0:T(8,128)(2,1)}) %all-gather.2.cloned.1.call-update) | async-done | bytes 14680080 | tf_op jit(solution)/shard_map/all_gather | solution.py:29
  205.7 0.0 copy-start.3
  205.7 0.0 slice-start
  205.7 13.4 %fusion.1 = f32[1024,512]{1,0:T(8,128)S(1)} fusion(bf16[1024,7168]{1,0:T(8,128)(2,1)} %bitcast.32, bf16[1,7168,512]{2,1,0:T(8,128)(2,1)} %param.10), kind=kOutput, calls=%fused_computation.4 | convolution fusion | flops 7516192768 | bytes 24117248 | tf_op jit(solution)/shard_map/dot_general | solution.py:37
  219.1 0.0 copy-done.3
  219.1 0.0 slice-start.1
  219.1 10.3 %multiply_convert_fusion = bf16[1024,512]{1,0:T(8,128)(2,1)S(1)} fusion(f32[1024,512]{1,0:T(8,128)S(1)} %fusion.1, bf16[1024,7168]{1,0:T(8,128)(2,1)S(1)} %bitcast.33, bf16[1,7168,512]{2,1,0:T(8,128)(2,1)} %param.9), kind=kOutput, calls=%fused_computation.8 | convolution fusion | flops 7519338496 | bytes 25165824 | tf_op jit(solution)/shard_map/dot_general | solution.py:36
  229.4 0.0 slice-done
  229.4 0.0 slice-done.1
  229.4 11.1 %convolution_convert_fusion = bf16[1024,7168]{1,0:T(8,128)(2,1)} fusion(bf16[1024,512]{1,0:T(8,128)(2,1)S(1)} %multiply_convert_fusion, bf16[1,512,7168]{2,1,0:T(8,128)(2,1)S(1)} %bitcast.35), kind=kOutput, calls=%fused_computation | convolution fusion | flops 7523532800 | bytes 23068672 | tf_op jit(solution)/shard_map/dot_general | solution.py:40
  240.5 0.0 reduce-scatter.2.cloned.1.call-update
  240.5 0.0 copy-start.2
  240.5 26.1 %reduce-scatter.2.cloned.1.call-done = bf16[8,64,7168]{2,1,0:T(8,128)(2,1)} async-done(((bf16[16,64,7168]{2,1,0:T(8,128)(2,1)}), bf16[8,64,7168]{2,1,0:T(8,128)(2,1)}) %reduce-scatter.2.cloned.1.call-update) | async-done | bytes 7340048 | tf_op jit(solution)/shard_map/reduce_scatter | solution.py:45
  266.7 5.9 %all-to-all-start.1 = ((bf16[8,64,7168]{2,1,0:T(8,128)(2,1)}), bf16[8,64,7168]{2,1,0:T(8,128)(2,1)}, u32[]{:S(2)}, u32[]{:S(2)}) async-start(bf16[8,64,7168]{2,1,0:T(8,128)(2,1)} %reduce-scatter.2.cloned.1.call-done), calls=%async_computation.2 | async-start | bytes 14680064 | tf_op jit(solution)/shard_map/all_to_all | solution.py:48
  272.6 0.0 copy-done.2
  272.6 0.0 copy-start.1
  272.6 0.1 select_reduce_fusion
  272.7 160.8 %all-to-all-done.1 = bf16[8,64,7168]{2,1,0:T(8,128)(2,1)} async-done(((bf16[8,64,7168]{2,1,0:T(8,128)(2,1)}), bf16[8,64,7168]{2,1,0:T(8,128)(2,1)}, u32[]{:S(2)}, u32[]{:S(2)}) %all-to-all-start.1) | async-done | bytes 7340064 | tf_op jit(solution)/shard_map/all_to_all | solution.py:48
  433.6 5.4 %convolution_convert_fusion.2 = bf16[64,7168]{1,0:T(8,128)(2,1)} fusion(bf16[512,7168]{1,0:T(8,128)(2,1)} %bitcast.8, bf16[64,512]{1,0:T(8,128)(2,1)S(1)} %select_reduce_fusion), kind=kOutput, calls=%fused_computation.2 | convolution fusion | flops 470220800 | bytes 8323072 | tf_op jit(solution)/shard_map/dot_general | solution.py:49
  439.0 0.0 copy-done.1
  (5 shorter events, 0.1 us)
Async XLA Ops:
  6.5 3.1 copy-start
  6.5 199.2 %all-gather.2.cloned.1.call-start = ((), (), s32[]{:S(2)}) async-start(), calls=%async_computation.3 | async-start | bytes 22020096 | tf_op jit(solution)/shard_map/all_gather | solution.py:29
  179.5 87.1 %reduce-scatter.2.cloned.1.call-start = ((), (), s32[]{:S(2)}) async-start(), calls=%async_computation.4 | async-start | bytes 22020096 | tf_op jit(solution)/shard_map/reduce_scatter | solution.py:45
  205.7 13.4 %copy-start.3 = (bf16[16,64,7168]{2,1,0:T(8,128)(2,1)S(1)}, bf16[16,64,7168]{2,1,0:T(8,128)(2,1)}, u32[]{:S(2)}) copy-start(bf16[16,64,7168]{2,1,0:T(8,128)(2,1)} %all-gather.2.cloned.1.call-done) | copy-start | bytes 44040196
  205.7 23.7 %slice-start = ((s8[7340032]{0:T(1024)(128)(4,1)}), s8[4194304]{0:T(1024)(128)(4,1)S(1)}, s32[]{:S(2)}) async-start(s8[7340032]{0:T(1024)(128)(4,1)} %bitcast.34), calls=%async_computation.5 | async-start | bytes 8388608
  219.1 10.3 %slice-start.1 = ((s8[7340032]{0:T(1024)(128)(4,1)}), s8[3145728]{0:T(1024)(128)(4,1)S(1)}, s32[]{:S(2)}) async-start(s8[7340032]{0:T(1024)(128)(4,1)} %bitcast.34), calls=%async_computation.6 | async-start | bytes 6291456
  240.5 32.1 %copy-start.2 = (bf16[64,4]{0,1:T(4,128)(2,1)S(1)}, bf16[64,4]{0,1:T(4,128)(2,1)}, u32[]{:S(2)}) copy-start(bf16[64,4]{0,1:T(4,128)(2,1)} %param.8) | copy-start | bytes 1540
  266.7 166.9 %all-to-all-start.1 = ((bf16[8,64,7168]{2,1,0:T(8,128)(2,1)}), bf16[8,64,7168]{2,1,0:T(8,128)(2,1)}, u32[]{:S(2)}, u32[]{:S(2)}) async-start(bf16[8,64,7168]{2,1,0:T(8,128)(2,1)} %reduce-scatter.2.cloned.1.call-done), calls=%async_computation.2 | async-start | bytes 14680064 | tf_op jit(solution)/shard_map/all_to_all | solution.py:48
  272.6 166.4 %copy-start.1 = (bf16[64,7168]{1,0:T(8,128)(2,1)S(1)}, bf16[64,7168]{1,0:T(8,128)(2,1)}, u32[]{:S(2)}) copy-start(bf16[64,7168]{1,0:T(8,128)(2,1)} %param.6) | copy-start | bytes 2752516
Sparse Core Ops, SparseCore 0:
  179.7 26.0 all-gather.1
  240.6 25.9 reduce-scatter.1
where the time goes:
time: 446 us
  waiting for transfers between devices  213 us (48%)
  blocking collectives  168 us (38%)
  matrix products  42.2 us (9%)
  between operations  13.5 us (3%)
  starting transfers between devices  5.94 us (1%)
    all_to_all x1, blocking collectives, per_device(): lax.all_to_all(outgoing, 'node', split_axis=0, concat_axis=0, tiled=True)  168 us
    all_to_all x1, waiting for transfers between devices, per_device(): lax.all_to_all(own_rows, 'node', split_axis=0, concat_axis=0, tiled=True)  161 us
    all_gather x1, waiting for transfers between devices, per_device(): lax.all_gather(lax.all_to_all(outgoing, 'node', split_axis=0, concat_axis...  26.1 us
    reduce_scatter x1, waiting for transfers between devices, per_device(): lax.psum_scatter(partial_value.astype(jnp.bfloat16), 'local', scatter_dim...  26.1 us
    dot_general x1, matrix products, per_device(): up_act = jnp.dot(rows, w_up[0], preferred_element_type=jnp.float32)  13.4 us
    dot_general x1, matrix products, per_device(): jnp.dot(hidden, w_down[0], preferred_element_type=jnp.float32)  11.1 us
    dot_general x1, matrix products, per_device(): gate_act = jnp.dot(rows, w_gate[0], preferred_element_type=jnp.float32)  10.3 us
  transfers between devices with their start and end apart: 3, of which 3 were waited for; matrix products, arithmetic and copies ran while one was open for 0% of the time, Pallas kernels for 0%

commit v1 on v0

v1 whole, which is shorter than its diff:
```python
import jax
import jax.numpy as jnp
from jax import lax
from jax.sharding import PartitionSpec as P


def per_device(tokens, gate_ids, gate_values, w_gate, w_up, w_down):
    node_count = lax.axis_size("node")
    expert_row = jnp.arange(node_count, dtype=jnp.int32)
    weight = jnp.sum(
        jnp.where(
            gate_ids[:, :, None] == expert_row[None, None, :],
            gate_values.astype(jnp.float32)[:, :, None],
            jnp.float32(0.0),
        ),
        axis=1,
    ).astype(jnp.bfloat16)
    every = ("node", "local")
    weights = lax.all_gather(weight, every, axis=0, tiled=True)
    rows = lax.all_gather(tokens, every, axis=0, tiled=True)
    mine = (expert_row == lax.axis_index("node"))[None, :]
    scale = jnp.sum(jnp.where(mine, weights.astype(jnp.float32), 0.0), axis=1, keepdims=True)
    gate_act = jnp.dot(rows, w_gate[0], preferred_element_type=jnp.float32)
    up_act = jnp.dot(rows, w_up[0], preferred_element_type=jnp.float32)
    hidden = (jax.nn.silu(gate_act) * up_act).astype(jnp.bfloat16)
    partial_value = jnp.dot(hidden, w_down[0], preferred_element_type=jnp.float32) * scale
    return lax.psum_scatter(
        partial_value.astype(jnp.bfloat16), every, scatter_dimension=0, tiled=True
    )


def solution(mesh):
    return jax.shard_map(
        per_device,
        mesh=mesh,
        in_specs=(
            P(("rep", "node", "local"), None),
            P(("rep", "node", "local"), None),
            P(("rep", "node", "local"), None),
            P("node", None, "local"),
            P("node", None, "local"),
            P("node", "local", None),
        ),
        out_specs=P(("rep", "node", "local"), None),
        check_vma=False,
    )
```

time: 446 us -> 316 us (0.71)
  blocking collectives: 168 us -> 23.7 us
  waiting for transfers between devices: 213 us -> 242 us
  matrix products: 42.2 us -> 34.5 us
  starting transfers between devices: 5.94 us -> 0.04 us
    all_to_all x1 -> x0, blocking collectives: 168 us -> none  [per_device(): lax.all_to_all(outgoing, 'node', split_axis=0, concat_axis=0, tiled=True)]
    all_to_all x1 -> x0, waiting for transfers between devices: 161 us -> none  [per_device(): lax.all_to_all(own_rows, 'node', split_axis=0, concat_axis=0, tiled=True)]
    reduce_scatter x1, waiting for transfers between devices: 26.1 us -> 148 us  [per_device(): lax.psum_scatter(partial_value.astype(jnp.bfloat16), every, scatter_dimen...]
    all_gather x1, waiting for transfers between devices: 26.1 us -> 93.2 us  [per_device(): rows = lax.all_gather(tokens, every, axis=0, tiled=True)]
    all_gather x0 -> x1, blocking collectives: none -> 23.7 us  [per_device(): weights = lax.all_gather(weight, every, axis=0, tiled=True)]
    dot_general x3 -> x1, matrix products: 18.6 us -> 11 us  [per_device(): jnp.dot(hidden, w_down[0], preferred_element_type=jnp.float32) * scale]
    all_to_all x1 -> x0, starting transfers between devices: 5.9 us -> none  [per_device(): lax.all_to_all(own_rows, 'node', split_axis=0, concat_axis=0, tiled=True)]
  transfers between devices with their start and end apart: 3 -> 2, of which waited for: 3 -> 2; matrix products, arithmetic and copies ran while one was open for 0% -> 0% of each run, Pallas kernels for 0% -> 0%
where the time goes in v1:
time: 316 us
  waiting for transfers between devices  242 us (77%)
  matrix products  34.5 us (11%)
  blocking collectives  23.7 us (8%)
  between operations  13.5 us (4%)
    reduce_scatter x1, waiting for transfers between devices, per_device(): lax.psum_scatter(partial_value.astype(jnp.bfloat16), every, scatter_dimen...  148 us
    all_gather x1, waiting for transfers between devices, per_device(): rows = lax.all_gather(tokens, every, axis=0, tiled=True)  93.2 us
    all_gather x1, blocking collectives, per_device(): weights = lax.all_gather(weight, every, axis=0, tiled=True)  23.7 us
    dot_general x1, matrix products, per_device(): up_act = jnp.dot(rows, w_up[0], preferred_element_type=jnp.float32)  13.3 us
    dot_general x1, matrix products, per_device(): jnp.dot(hidden, w_down[0], preferred_element_type=jnp.float32) * scale  11 us
    dot_general x1, matrix products, per_device(): gate_act = jnp.dot(rows, w_gate[0], preferred_element_type=jnp.float32)  10.2 us
  transfers between devices with their start and end apart: 2, of which 2 were waited for; matrix products, arithmetic and copies ran while one was open for 0% of the time, Pallas kernels for 0%

profile of v1, /device:TPU:0, one launch (start us, length us, event | category | flops | bytes accessed | tf_op | source)
XLA Modules:
  0.0 315.6 jit_solution(5433363231645133118)
XLA Ops:
  6.5 0.0 all-gather.3.cloned.1.call-start
  6.5 0.7 all-gather.3.cloned.1.call-update
  7.3 0.0 reduce-scatter.2.cloned.1.call-start
  7.3 0.7 convert_element_type.16
  8.0 0.7 select_reduce_fusion.1
  8.7 23.7 %all-gather = bf16[16,64,8]{1,2,0:T(8,128)(2,1)S(1)} all-gather(bf16[1,64,8]{1,2,0:T(8,128)(2,1)S(1)} %bitcast.19), channel_id=1, replica_groups=mesh['rep'=2,'node'=8,'local'=2] {'node','local'}, dimensions={0}, use_global_device_ids=true | all-gather | bytes 17408 | tf_op jit(solution)/shard_map/all_gather | solution.py:19
  32.4 0.1 reshape.9
  32.5 0.1 select_reduce_fusion
  32.6 93.2 %all-gather.3.cloned.1.call-done = bf16[1024,7168]{1,0:T(8,128)(2,1)} async-done(((bf16[64,7168]{1,0:T(8,128)(2,1)}), bf16[1024,7168]{1,0:T(8,128)(2,1)}) %all-gather.3.cloned.1.call-update) | async-done | bytes 14680080 | tf_op jit(solution)/shard_map/all_gather | solution.py:20
  125.8 0.0 copy-start
  125.8 0.0 slice-start
  125.8 13.3 %fusion.1 = f32[1024,512]{1,0:T(8,128)S(1)} fusion(bf16[1024,7168]{1,0:T(8,128)(2,1)} %all-gather.3.cloned.1.call-done, bf16[1,7168,512]{2,1,0:T(8,128)(2,1)} %param.10), kind=kOutput, calls=%fused_computation.2 | convolution fusion | flops 7516192768 | bytes 24117248 | tf_op jit(solution)/shard_map/dot_general | solution.py:24
  139.1 0.0 copy-done
  139.1 0.0 slice-start.1
  139.1 10.2 %multiply_convert_fusion.1 = bf16[1024,512]{1,0:T(8,128)(2,1)S(1)} fusion(f32[1024,512]{1,0:T(8,128)S(1)} %fusion.1, bf16[1024,7168]{1,0:T(8,128)(2,1)S(1)} %copy-done, bf16[1,7168,512]{2,1,0:T(8,128)(2,1)} %param.9), kind=kOutput, calls=%fused_computation.6 | convolution fusion | flops 7519338496 | bytes 25165824 | tf_op jit(solution)/shard_map/dot_general | solution.py:23
  149.4 0.0 slice-done
  149.4 0.0 slice-done.1
  149.4 11.0 %multiply_convert_fusion = bf16[1024,7168]{1,0:T(8,128)(2,1)} fusion(bf16[1024,512]{1,0:T(8,128)(2,1)S(1)} %multiply_convert_fusion.1, f32[1024]{0:T(1024)S(1)} %select_reduce_fusion, bf16[1,512,7168]{2,1,0:T(8,128)(2,1)S(1)} %bitcast.21), kind=kOutput, calls=%fused_computation | convolution fusion | flops 7530872832 | bytes 23072768 | tf_op jit(solution)/shard_map/dot_general | solution.py:26
  160.4 0.0 reduce-scatter.2.cloned.1.call-update
  160.4 148.4 %reduce-scatter.2.cloned.1.call-done = bf16[64,7168]{1,0:T(8,128)(2,1)} async-done(((bf16[1024,7168]{1,0:T(8,128)(2,1)}), bf16[64,7168]{1,0:T(8,128)(2,1)}) %reduce-scatter.2.cloned.1.call-update) | async-done | bytes 917520 | tf_op jit(solution)/shard_map/reduce_scatter | solution.py:27
  (3 shorter events, 0.0 us)
Async XLA Ops:
  6.5 119.2 %all-gather.3.cloned.1.call-start = ((), (), s32[]{:S(2)}) async-start(), calls=%async_computation.1 | async-start | bytes 15597568 | tf_op jit(solution)/shard_map/all_gather | solution.py:20
  7.3 301.5 %reduce-scatter.2.cloned.1.call-start = ((), (), s32[]{:S(2)}) async-start(), calls=%async_computation.2 | async-start | bytes 15597568 | tf_op jit(solution)/shard_map/reduce_scatter | solution.py:27
  125.8 13.4 %copy-start = (bf16[1024,7168]{1,0:T(8,128)(2,1)S(1)}, bf16[1024,7168]{1,0:T(8,128)(2,1)}, u32[]{:S(2)}) copy-start(bf16[1024,7168]{1,0:T(8,128)(2,1)} %all-gather.3.cloned.1.call-done) | copy-start | bytes 44040196
  125.8 23.6 %slice-start = ((s8[7340032]{0:T(1024)(128)(4,1)}), s8[4194304]{0:T(1024)(128)(4,1)S(1)}, s32[]{:S(2)}) async-start(s8[7340032]{0:T(1024)(128)(4,1)} %bitcast.20), calls=%async_computation.3 | async-start | bytes 8388608
  139.1 10.3 %slice-start.1 = ((s8[7340032]{0:T(1024)(128)(4,1)}), s8[3145728]{0:T(1024)(128)(4,1)S(1)}, s32[]{:S(2)}) async-start(s8[7340032]{0:T(1024)(128)(4,1)} %bitcast.20), calls=%async_computation.4 | async-start | bytes 6291456
Sparse Core Ops, SparseCore 0:
  9.6 116.0 all-gather.2
  160.5 148.2 reduce-scatter.1

commit v2 on v1

v2 whole, which is shorter than its diff:
```python
import functools

import jax
import jax.numpy as jnp
from jax import lax
from jax.experimental import pallas as pl
from jax.experimental.pallas import tpu as pltpu
from jax.sharding import PartitionSpec as P

MESH = pl.DeviceIdType.MESH
LANES = 128
VMEM_LIMIT = 67_000_000


def chunk_of(size, most=1024):
    chunk = most
    while size % chunk:
        chunk -= LANES
    return chunk


def expert_weights(gate_ids, gate_values, columns):
    expert_row = jnp.arange(columns, dtype=jnp.int32)
    return jnp.sum(
        jnp.where(
            gate_ids[:, :, None] == expert_row[None, None, :],
            gate_values.astype(jnp.float32)[:, :, None],
            jnp.float32(0.0),
        ),
        axis=1,
    ).astype(jnp.bfloat16)


def ring_kernel(
    n, block, wg_hbm, wu_hbm, wd_hbm, out,
    x, wg, wu, wd, ring_in, pin, pout, acc, own, gate_acc, up_acc,
    weight_sem, own_sem, ag_send, ag_recv, pa_send, pa_recv,
    pp_send, pp_recv, rs_send, rs_recv,
):
    tok, wide = block.shape
    width = wg.shape[0]
    half = tok // 2
    depth = n // 2
    node = lax.axis_index("node")
    partner = 1 - lax.axis_index("local")
    row, column = node // 2, node % 2
    place = row * (1 - column) + (n - 1 - row) * column

    def node_at(position):
        side = position // depth
        level = position * (1 - side) + (n - 1 - position) * side
        return 2 * level + side

    to = (node_at((place + 1) % n), node_at((place + n - 1) % n))

    loads = [
        pltpu.make_async_copy(src, dst, weight_sem.at[k])
        for k, (src, dst) in enumerate(((wg_hbm, wg), (wu_hbm, wu), (wd_hbm, wd)))
    ]
    keep = pltpu.make_async_copy(block, x.at[0, pl.ds(0, tok)], own_sem.at[0])

    barrier = pltpu.get_barrier_semaphore()
    for target in ({"node": to[0]}, {"node": to[1]}, {"local": partner}):
        pl.semaphore_signal(barrier, inc=1, device_id=target, device_id_type=MESH)
    pl.semaphore_wait(barrier, 3)

    def rows_of(d):
        return pl.ds(d * half, half)

    def ag(step, d, src):
        return pltpu.make_async_remote_copy(
            src_ref=src, dst_ref=x.at[step, rows_of(d)],
            send_sem=ag_send.at[step, d], recv_sem=ag_recv.at[step, d],
            device_id={"node": to[d]}, device_id_type=MESH,
        )

    def pa(step, src):
        return pltpu.make_async_remote_copy(
            src_ref=src, dst_ref=x.at[step, pl.ds(tok, tok)],
            send_sem=pa_send.at[step], recv_sem=pa_recv.at[step],
            device_id={"local": partner}, device_id_type=MESH,
        )

    def pp(step, slot):
        return pltpu.make_async_remote_copy(
            src_ref=pout.at[slot], dst_ref=pin.at[step],
            send_sem=pp_send.at[slot], recv_sem=pp_recv.at[step],
            device_id={"local": partner}, device_id_type=MESH,
        )

    def rs(i, d, slot):
        return pltpu.make_async_remote_copy(
            src_ref=acc.at[slot, rows_of(d)], dst_ref=ring_in.at[i - 1, rows_of(d)],
            send_sem=rs_send.at[slot, d], recv_sem=rs_recv.at[i - 1, d],
            device_id={"node": to[d]}, device_id_type=MESH,
        )

    ag(1, 0, block.at[rows_of(0)]).start()
    ag(1, 1, block.at[rows_of(1)]).start()
    for load in loads:
        load.start()
    pa(0, block).start()
    keep.start()

    kc = chunk_of(width)

    def compute(step, slot):
        gate_acc[...] = jnp.zeros_like(gate_acc)
        up_acc[...] = jnp.zeros_like(up_acc)

        @pl.loop(0, width // kc)
        def _(k):
            cols = pl.ds(pl.multiple_of(k * kc, LANES), kc)
            rows = x[step, :, cols]
            gate_acc[...] += jnp.dot(rows, wg[cols, :], preferred_element_type=jnp.float32)
            up_acc[...] += jnp.dot(rows, wu[cols, :], preferred_element_type=jnp.float32)

        gate = gate_acc[...]
        hidden = (gate / (1.0 + jnp.exp(-gate)) * up_acc[...]).astype(jnp.bfloat16)
        table = x[step, :, pl.ds(width, LANES)].astype(jnp.float32)
        lane = lax.broadcasted_iota(jnp.int32, table.shape, 1)
        scale = jnp.sum(jnp.where(lane == node, table, 0.0), axis=1, keepdims=True)

        @pl.loop(0, width // kc)
        def _(k):
            cols = pl.ds(pl.multiple_of(k * kc, LANES), kc)
            value = jnp.dot(hidden, wd[:, cols], preferred_element_type=jnp.float32) * scale
            own[:, cols] = value[:tok]
            pout[slot, :, cols] = value[tok:].astype(jnp.bfloat16)

    def combine(step, i, d, dst, first):
        @pl.loop(0, width // kc)
        def _(k):
            cols = pl.ds(pl.multiple_of(k * kc, LANES), kc)
            value = own[rows_of(d), cols] + pin[step, rows_of(d), cols].astype(jnp.float32)
            if not first:
                value += ring_in[i - 2, rows_of(d), cols].astype(jnp.float32)
            dst[rows_of(d), cols] = value.astype(jnp.bfloat16)

    def gather_step(i, forward):
        for d in range(2):
            ag(i, d, block.at[rows_of(d)]).wait_recv()
            if forward:
                ag(i + 1, d, x.at[i, rows_of(d)]).start()
        pa(i, x.at[i, pl.ds(0, tok)]).start()
        pa(i, x.at[i, pl.ds(0, tok)]).wait_recv()

    def reduce_step(i, first):
        slot = i % 2
        pp(i, slot).start()
        pp(i, slot).wait_recv()
        for d in range(2):
            if not first:
                rs(i - 1, d, slot).wait_recv()
            combine(i, i, d, acc.at[slot], first)
            rs(i, d, slot).start()

    def free_slot(i):
        slot = i % 2

        @pl.when(i >= 3)
        def _():
            pp(i, slot).wait_send()
            for d in range(2):
                rs(i, d, slot).wait_send()

    gather_step(1, True)
    for load in loads:
        load.wait()
    compute(1, 1)
    reduce_step(1, True)

    @pl.loop(2, n - 1)
    def _(i):
        gather_step(i, True)
        free_slot(i)
        compute(i, i % 2)
        reduce_step(i, False)

    gather_step(n - 1, False)
    free_slot(n - 1)
    compute(n - 1, (n - 1) % 2)
    reduce_step(n - 1, False)

    last = n % 2
    keep.wait()
    pa(0, block).wait_recv()
    pp(0, last).wait_send()
    compute(0, last)
    pp(0, last).start()
    pp(0, last).wait_recv()
    for d in range(2):
        rs(n - 1, d, last).wait_recv()
        combine(0, n, d, out, False)
    for d in range(2):
        for slot in range(2):
            rs(1, d, slot).wait_send()

        @pl.loop(1, n)
        def _(i):
            ag(i, d, block.at[rows_of(d)]).wait_send()

    for slot in range(2):
        pp(0, slot).wait_send()

    @pl.loop(0, n)
    def _(i):
        pa(i, block).wait_send()


def by_ring(n, tokens, gate_ids, gate_values, w_gate, w_up, w_down):
    tok, width = tokens.shape
    hid = w_gate.shape[2]
    half_type = jnp.bfloat16
    block = jnp.concatenate([tokens, expert_weights(gate_ids, gate_values, LANES)], axis=1)
    anywhere = pl.BlockSpec(memory_space=pl.ANY)
    dma = pltpu.SemaphoreType.DMA
    return pl.pallas_call(
        functools.partial(ring_kernel, n),
        out_shape=jax.ShapeDtypeStruct((tok, width), half_type),
        in_specs=[anywhere] * 4,
        out_specs=pl.BlockSpec(memory_space=pltpu.VMEM),
        scratch_shapes=[
            pltpu.VMEM((n, 2 * tok, width + LANES), half_type),
            pltpu.VMEM((width, hid), half_type),
            pltpu.VMEM((width, hid), half_type),
            pltpu.VMEM((hid, width), half_type),
            pltpu.VMEM((n - 1, tok, width), half_type),
            pltpu.VMEM((n, tok, width), half_type),
            pltpu.VMEM((2, tok, width), half_type),
            pltpu.VMEM((2, tok, width), half_type),
            pltpu.VMEM((tok, width), jnp.float32),
            pltpu.VMEM((2 * tok, hid), jnp.float32),
            pltpu.VMEM((2 * tok, hid), jnp.float32),
            dma((3,)), dma((1,)), dma((n, 2)), dma((n, 2)), dma((n,)), dma((n,)),
            dma((2,)), dma((n,)), dma((2, 2)), dma((n - 1, 2)),
        ],
        compiler_params=pltpu.CompilerParams(
            collective_id=0, has_side_effects=True, vmem_limit_bytes=VMEM_LIMIT
        ),
    )(block, w_gate[0], w_up[0], w_down[0])


def by_collectives(tokens, gate_ids, gate_values, w_gate, w_up, w_down):
    n = lax.axis_size("node")
    every = ("node", "local")
    weights = lax.all_gather(expert_weights(gate_ids, gate_values, n), every, axis=0, tiled=True)
    rows = lax.all_gather(tokens, every, axis=0, tiled=True)
    mine = (jnp.arange(n, dtype=jnp.int32) == lax.axis_index("node"))[None, :]
    scale = jnp.sum(jnp.where(mine, weights.astype(jnp.float32), 0.0), axis=1, keepdims=True)
    gate_act = jnp.dot(rows, w_gate[0], preferred_element_type=jnp.float32)
    up_act = jnp.dot(rows, w_up[0], preferred_element_type=jnp.float32)
    hidden = (jax.nn.silu(gate_act) * up_act).astype(jnp.bfloat16)
    partial_value = jnp.dot(hidden, w_down[0], preferred_element_type=jnp.float32) * scale
    return lax.psum_scatter(
        partial_value.astype(jnp.bfloat16), every, scatter_dimension=0, tiled=True
    )


def ring_fits(n, tok, width, hid):
    rows = n * 2 * tok + (n - 1) * tok + n * tok + 7 * tok
    return 2 * width * (rows + 3 * hid) + 8 * 2 * tok * hid + 2**21 < VMEM_LIMIT


def per_device(tokens, gate_ids, gate_values, w_gate, w_up, w_down):
    n = lax.axis_size("node")
    fits = ring_fits(n, tokens.shape[0], tokens.shape[1], w_gate.shape[2])
    if n % 2 == 0 and n >= 4 and lax.axis_size("local") == 2 and n <= LANES and fits:
        return by_ring(n, tokens, gate_ids, gate_values, w_gate, w_up, w_down)
    return by_collectives(tokens, gate_ids, gate_values, w_gate, w_up, w_down)


def solution(mesh):
    return jax.shard_map(
        per_device,
        mesh=mesh,
        in_specs=(
            P(("rep", "node", "local"), None),
            P(("rep", "node", "local"), None),
            P(("rep", "node", "local"), None),
            P("node", None, "local"),
            P("node", None, "local"),
            P("node", "local", None),
        ),
        out_specs=P(("rep", "node", "local"), None),
        check_vma=False,
    )
```

time: 316 us -> 156 us (0.49)
  waiting for transfers between devices: 242 us -> 0 us
  Pallas kernels: 0 us -> 150 us
  matrix products: 34.5 us -> 0 us
  blocking collectives: 23.7 us -> 0 us
  between operations: 13.5 us -> 0.01 us
    pallas_call x0 -> x1, Pallas kernels: none -> 150 us  [by_ring(): pl.pallas_call(functools.partial(ring_kernel, n), out_shape=jax.ShapeDtyp...]
    reduce_scatter x1 -> x0, waiting for transfers between devices: 148 us -> none  [per_device(): lax.psum_scatter(partial_value.astype(jnp.bfloat16), every, scatter_dimen...]
    all_gather x1 -> x0, waiting for transfers between devices: 93.2 us -> none  [per_device(): rows = lax.all_gather(tokens, every, axis=0, tiled=True)]
    dot_general x3 -> x0, matrix products: 34.5 us -> none  [the longest x1 13.3 us: per_device(): up_act = jnp.dot(rows, w_up[0], preferred_element_type=jnp.float32)]
    all_gather x1 -> x0, blocking collectives: 23.7 us -> none  [per_device(): weights = lax.all_gather(weight, every, axis=0, tiled=True)]
  transfers between devices with their start and end apart: 2 -> 0, of which waited for: 2 -> 0; matrix products, arithmetic and copies ran while one was open for 0% -> 0% of each run, Pallas kernels for 0% -> 0%
where the time goes in v2:
time: 156 us
  Pallas kernels  150 us (96%)
  other arithmetic  3.67 us (2%)
  local copies, waits for them, and re-layouts  2.16 us (1%)
    pallas_call x1, Pallas kernels, by_ring(): pl.pallas_call(functools.partial(ring_kernel, n), out_shape=jax.ShapeDtyp...  150 us

profile of v2, /device:TPU:0, one launch (start us, length us, event | category | flops | bytes accessed | tf_op | source)
XLA Modules:
  0.0 156.0 jit_solution(8586720796755020598)
XLA Ops:
  0.0 0.7 convert_element_type.6
  0.7 0.8 select_reduce_fusion
  1.5 2.2 %pad_maximum_fusion.block = bf16[64,7296]{1,0:T(8,128)(2,1)} fusion(bf16[64,128]{1,0:T(8,128)(2,1)S(1)} %select_reduce_fusion, bf16[64,7168]{1,0:T(8,128)(2,1)} %param.6), kind=kLoop, calls=%fused_computation | loop fusion | flops 1867776 | bytes 1867776 | tf_op jit(solution)/shard_map/concatenate | solution.py:215
  3.7 150.2 %shard_map.64 = bf16[64,7168]{1,0:T(8,128)(2,1)} custom-call(bf16[64,7296]{1,0:T(8,128)(2,1)} %pad_maximum_fusion.block, bf16[7168,512]{1,0:T(8,128)(2,1)} %bitcast.3, bf16[7168,512]{1,0:T(8,128)(2,1)} %bitcast.4, bf16[512,7168]{1,0:T(8,128)(2,1)} %bitcast.5), custom_call_target="tpu_custom_call" | custom-call | tf_op jit(solution)/shard_map/pallas_call | solution.py:218
  153.9 2.2 %copy.10 = bf16[64,7168]{1,0:T(8,128)(2,1)} copy(bf16[64,7168]{1,0:T(8,128)(2,1)} %shard_map.64) | data formatting | bytes 1835008

commit v3 on v2

--- a/solution.py
+++ b/solution.py
@@ -32,13 +32,12 @@
 
 
 def ring_kernel(
-    n, block, wg_hbm, wu_hbm, wd_hbm, out,
+    n, tokens, ids, values, wg_hbm, wu_hbm, wd_hbm, out,
     x, wg, wu, wd, ring_in, pin, pout, acc, own, gate_acc, up_acc,
     weight_sem, own_sem, ag_send, ag_recv, pa_send, pa_recv,
     pp_send, pp_recv, rs_send, rs_recv,
 ):
-    tok, wide = block.shape
-    width = wg.shape[0]
+    tok, width = tokens.shape
     half = tok // 2
     depth = n // 2
     node = lax.axis_index("node")
@@ -57,11 +56,21 @@
         pltpu.make_async_copy(src, dst, weight_sem.at[k])
         for k, (src, dst) in enumerate(((wg_hbm, wg), (wu_hbm, wu), (wd_hbm, wd)))
     ]
-    keep = pltpu.make_async_copy(block, x.at[0, pl.ds(0, tok)], own_sem.at[0])
+    keep = pltpu.make_async_copy(
+        tokens, x.at[0, pl.ds(0, tok), pl.ds(0, width)], own_sem.at[0]
+    )
+    keep.start()
 
     barrier = pltpu.get_barrier_semaphore()
     for target in ({"node": to[0]}, {"node": to[1]}, {"local": partner}):
         pl.semaphore_signal(barrier, inc=1, device_id=target, device_id_type=MESH)
+    table_lane = lax.broadcasted_iota(jnp.int32, (tok, LANES), 1)
+    table = jnp.zeros((tok, LANES), jnp.float32)
+    for choice in range(ids.shape[1]):
+        chosen = table_lane == ids[:, pl.ds(choice, 1)]
+        table += jnp.where(chosen, values[:, pl.ds(choice, 1)].astype(jnp.float32), 0.0)
+    x[0, pl.ds(0, tok), pl.ds(width, LANES)] = table.astype(jnp.bfloat16)
+    keep.wait()
     pl.semaphore_wait(barrier, 3)
 
     def rows_of(d):
@@ -95,12 +104,11 @@
             device_id={"node": to[d]}, device_id_type=MESH,
         )
 
-    ag(1, 0, block.at[rows_of(0)]).start()
-    ag(1, 1, block.at[rows_of(1)]).start()
+    for d in range(2):
+        ag(1, d, x.at[0, rows_of(d)]).start()
     for load in loads:
         load.start()
-    pa(0, block).start()
-    keep.start()
+    pa(0, x.at[0, pl.ds(0, tok)]).start()
 
     kc = chunk_of(width)
 
@@ -139,15 +147,18 @@
 
     def gather_step(i, forward):
         for d in range(2):
-            ag(i, d, block.at[rows_of(d)]).wait_recv()
+            ag(i, d, x.at[0, rows_of(d)]).wait_recv()
             if forward:
                 ag(i + 1, d, x.at[i, rows_of(d)]).start()
         pa(i, x.at[i, pl.ds(0, tok)]).start()
+
+    def compute_step(i):
         pa(i, x.at[i, pl.ds(0, tok)]).wait_recv()
+        compute(i, i % 2)
+        pp(i, i % 2).start()
 
     def reduce_step(i, first):
         slot = i % 2
-        pp(i, slot).start()
         pp(i, slot).wait_recv()
         for d in range(2):
             if not first:
@@ -167,24 +178,27 @@
     gather_step(1, True)
     for load in loads:
         load.wait()
-    compute(1, 1)
+    compute_step(1)
+    gather_step(2, True)
     reduce_step(1, True)
 
-    @pl.loop(2, n - 1)
+    @pl.loop(2, n - 2)
     def _(i):
-        gather_step(i, True)
         free_slot(i)
-        compute(i, i % 2)
+        compute_step(i)
+        gather_step(i + 1, True)
         reduce_step(i, False)
 
+    free_slot(n - 2)
+    compute_step(n - 2)
     gather_step(n - 1, False)
+    reduce_step(n - 2, False)
     free_slot(n - 1)
-    compute(n - 1, (n - 1) % 2)
+    compute_step(n - 1)
     reduce_step(n - 1, False)
 
     last = n % 2
-    keep.wait()
-    pa(0, block).wait_recv()
+    pa(0, x.at[0, pl.ds(0, tok)]).wait_recv()
     pp(0, last).wait_send()
     compute(0, last)
     pp(0, last).start()
@@ -198,27 +212,27 @@
 
         @pl.loop(1, n)
         def _(i):
-            ag(i, d, block.at[rows_of(d)]).wait_send()
+            ag(i, d, x.at[0, rows_of(d)]).wait_send()
 
     for slot in range(2):
         pp(0, slot).wait_send()
 
     @pl.loop(0, n)
     def _(i):
-        pa(i, block).wait_send()
+        pa(i, x.at[0, pl.ds(0, tok)]).wait_send()
 
 
 def by_ring(n, tokens, gate_ids, gate_values, w_gate, w_up, w_down):
     tok, width = tokens.shape
     hid = w_gate.shape[2]
     half_type = jnp.bfloat16
-    block = jnp.concatenate([tokens, expert_weights(gate_ids, gate_values, LANES)], axis=1)
     anywhere = pl.BlockSpec(memory_space=pl.ANY)
+    in_vmem = pl.BlockSpec(memory_space=pltpu.VMEM)
     dma = pltpu.SemaphoreType.DMA
     return pl.pallas_call(
         functools.partial(ring_kernel, n),
         out_shape=jax.ShapeDtypeStruct((tok, width), half_type),
-        in_specs=[anywhere] * 4,
+        in_specs=[anywhere, in_vmem, in_vmem, anywhere, anywhere, anywhere],
         out_specs=pl.BlockSpec(memory_space=pltpu.VMEM),
         scratch_shapes=[
             pltpu.VMEM((n, 2 * tok, width + LANES), half_type),
@@ -238,7 +252,7 @@
         compiler_params=pltpu.CompilerParams(
             collective_id=0, has_side_effects=True, vmem_limit_bytes=VMEM_LIMIT
         ),
-    )(block, w_gate[0], w_up[0], w_down[0])
+    )(tokens, gate_ids, gate_values, w_gate[0], w_up[0], w_down[0])
 
 
 def by_collectives(tokens, gate_ids, gate_values, w_gate, w_up, w_down):

time: 156 us -> 156 us (level)
  other arithmetic: 3.67 us -> 0 us
  local copies, waits for them, and re-layouts: 2.16 us -> 4.92 us
    unnamed x1 -> x3, local copies, waits for them, and re-layouts: 2.16 us -> 4.92 us
    concatenate x1 -> x0, other arithmetic: 2.18 us -> none  [by_ring(): jnp.concatenate([tokens, expert_weights(gate_ids, gate_values, LANES)], a...]
where the time goes in v3:
time: 156 us
  Pallas kernels  151 us (97%)
  local copies, waits for them, and re-layouts  4.92 us (3%)
    pallas_call x1, Pallas kernels, by_ring(): pl.pallas_call(functools.partial(ring_kernel, n), out_shape=jax.ShapeDtyp...  151 us
    unnamed x3, local copies, waits for them, and re-layouts  4.92 us

profile of v3, /device:TPU:0, one launch (start us, length us, event | category | flops | bytes accessed | tf_op | source)
XLA Modules:
  0.0 155.8 jit_solution(14630687300693399482)
XLA Ops:
  0.0 1.4 copy.8.values
  1.4 1.4 copy.7.ids
  2.8 150.9 %shard_map.64 = bf16[64,7168]{1,0:T(8,128)(2,1)} custom-call(bf16[64,7168]{1,0:T(8,128)(2,1)} %tokens.1, s32[64,4]{1,0:T(8,128)} %copy.7.ids, bf16[64,4]{1,0:T(8,128)(2,1)} %copy.8.values, bf16[7168,512]{1,0:T(8,128)(2,1)} %bitcast.3, bf16[7168,512]{1,0:T(8,128)(2,1)} %bitcast.4, bf16[512,7168]{1,0:T(8,128)(2,1)} %bitcast.5), custom_call_target="tpu_custom_call" | custom-call | tf_op jit(solution)/shard_map/pallas_call | solution.py:232
  153.7 2.2 %copy.10 = bf16[64,7168]{1,0:T(8,128)(2,1)} copy(bf16[64,7168]{1,0:T(8,128)(2,1)} %shard_map.64) | data formatting | bytes 1835008

commit v4 on v3

--- a/solution.py
+++ b/solution.py
@@ -9,6 +9,8 @@
 
 MESH = pl.DeviceIdType.MESH
 LANES = 128
+PARTS = 4
+ORDER = (0, 2, 1, 3)
 VMEM_LIMIT = 67_000_000
 
 
@@ -38,7 +40,7 @@
     pp_send, pp_recv, rs_send, rs_recv,
 ):
     tok, width = tokens.shape
-    half = tok // 2
+    part = tok // PARTS
     depth = n // 2
     node = lax.axis_index("node")
     partner = 1 - lax.axis_index("local")
@@ -64,23 +66,30 @@
     barrier = pltpu.get_barrier_semaphore()
     for target in ({"node": to[0]}, {"node": to[1]}, {"local": partner}):
         pl.semaphore_signal(barrier, inc=1, device_id=target, device_id_type=MESH)
-    table_lane = lax.broadcasted_iota(jnp.int32, (tok, LANES), 1)
-    table = jnp.zeros((tok, LANES), jnp.float32)
-    for choice in range(ids.shape[1]):
-        chosen = table_lane == ids[:, pl.ds(choice, 1)]
-        table += jnp.where(chosen, values[:, pl.ds(choice, 1)].astype(jnp.float32), 0.0)
+    table_row = lax.broadcasted_iota(jnp.int32, (LANES, tok), 0)
+    turned = jnp.zeros((LANES, tok), jnp.float32)
+    for choice in range(ids.shape[0]):
+        chosen = table_row == ids[pl.ds(choice, 1), :]
+        turned += jnp.where(chosen, values[pl.ds(choice, 1), :].astype(jnp.float32), 0.0)
+    ones = lax.broadcasted_iota(jnp.int32, (tok, tok), 0) == lax.broadcasted_iota(
+        jnp.int32, (tok, tok), 1
+    )
+    table = lax.dot_general(
+        jnp.where(ones, 1.0, 0.0).astype(jnp.bfloat16), turned.astype(jnp.bfloat16),
+        (((1,), (1,)), ((), ())), preferred_element_type=jnp.float32,
+    )
     x[0, pl.ds(0, tok), pl.ds(width, LANES)] = table.astype(jnp.bfloat16)
     keep.wait()
     pl.semaphore_wait(barrier, 3)
 
     def rows_of(d):
-        return pl.ds(d * half, half)
+        return pl.ds(d * part, part)
 
     def ag(step, d, src):
         return pltpu.make_async_remote_copy(
             src_ref=src, dst_ref=x.at[step, rows_of(d)],
             send_sem=ag_send.at[step, d], recv_sem=ag_recv.at[step, d],
-            device_id={"node": to[d]}, device_id_type=MESH,
+            device_id={"node": to[d // 2]}, device_id_type=MESH,
         )
 
     def pa(step, src):
@@ -101,10 +110,10 @@
         return pltpu.make_async_remote_copy(
             src_ref=acc.at[slot, rows_of(d)], dst_ref=ring_in.at[i - 1, rows_of(d)],
             send_sem=rs_send.at[slot, d], recv_sem=rs_recv.at[i - 1, d],
-            device_id={"node": to[d]}, device_id_type=MESH,
+            device_id={"node": to[d // 2]}, device_id_type=MESH,
         )
 
-    for d in range(2):
+    for d in ORDER:
         ag(1, d, x.at[0, rows_of(d)]).start()
     for load in loads:
         load.start()
@@ -146,7 +155,7 @@
             dst[rows_of(d), cols] = value.astype(jnp.bfloat16)
 
     def gather_step(i, forward):
-        for d in range(2):
+        for d in ORDER:
             ag(i, d, x.at[0, rows_of(d)]).wait_recv()
             if forward:
                 ag(i + 1, d, x.at[i, rows_of(d)]).start()
@@ -160,7 +169,7 @@
     def reduce_step(i, first):
         slot = i % 2
         pp(i, slot).wait_recv()
-        for d in range(2):
+        for d in ORDER:
             if not first:
                 rs(i - 1, d, slot).wait_recv()
             combine(i, i, d, acc.at[slot], first)
@@ -172,7 +181,7 @@
         @pl.when(i >= 3)
         def _():
             pp(i, slot).wait_send()
-            for d in range(2):
+            for d in ORDER:
                 rs(i, d, slot).wait_send()
 
     gather_step(1, True)
@@ -203,10 +212,10 @@
     compute(0, last)
     pp(0, last).start()
     pp(0, last).wait_recv()
-    for d in range(2):
+    for d in ORDER:
         rs(n - 1, d, last).wait_recv()
         combine(0, n, d, out, False)
-    for d in range(2):
+    for d in ORDER:
         for slot in range(2):
             rs(1, d, slot).wait_send()
 
@@ -246,13 +255,13 @@
             pltpu.VMEM((tok, width), jnp.float32),
             pltpu.VMEM((2 * tok, hid), jnp.float32),
             pltpu.VMEM((2 * tok, hid), jnp.float32),
-            dma((3,)), dma((1,)), dma((n, 2)), dma((n, 2)), dma((n,)), dma((n,)),
-            dma((2,)), dma((n,)), dma((2, 2)), dma((n - 1, 2)),
+            dma((3,)), dma((1,)), dma((n, PARTS)), dma((n, PARTS)), dma((n,)), dma((n,)),
+            dma((2,)), dma((n,)), dma((2, PARTS)), dma((n - 1, PARTS)),
         ],
         compiler_params=pltpu.CompilerParams(
             collective_id=0, has_side_effects=True, vmem_limit_bytes=VMEM_LIMIT
         ),
-    )(tokens, gate_ids, gate_values, w_gate[0], w_up[0], w_down[0])
+    )(tokens, gate_ids.T, gate_values.T, w_gate[0], w_up[0], w_down[0])
 
 
 def by_collectives(tokens, gate_ids, gate_values, w_gate, w_up, w_down):
@@ -279,7 +288,7 @@
 def per_device(tokens, gate_ids, gate_values, w_gate, w_up, w_down):
     n = lax.axis_size("node")
     fits = ring_fits(n, tokens.shape[0], tokens.shape[1], w_gate.shape[2])
-    if n % 2 == 0 and n >= 4 and lax.axis_size("local") == 2 and n <= LANES and fits:
+    if n % 2 == 0 and n >= 4 and tokens.shape[0] % 64 == 0 and lax.axis_size("local") == 2 and n <= LANES and fits:
         return by_ring(n, tokens, gate_ids, gate_values, w_gate, w_up, w_down)
     return by_collectives(tokens, gate_ids, gate_values, w_gate, w_up, w_down)
 

time: 156 us -> 149 us (0.955)
  Pallas kernels: 151 us -> 147 us
  local copies, waits for them, and re-layouts: 4.92 us -> 2.16 us
    pallas_call x1, Pallas kernels: 151 us -> 147 us  [by_ring(): pl.pallas_call(functools.partial(ring_kernel, n), out_shape=jax.ShapeDtyp...]
    unnamed x3 -> x1, local copies, waits for them, and re-layouts: 4.92 us -> 2.16 us
where the time goes in v4:
time: 149 us
  Pallas kernels  147 us (99%)
  local copies, waits for them, and re-layouts  2.16 us (1%)
    pallas_call x1, Pallas kernels, by_ring(): pl.pallas_call(functools.partial(ring_kernel, n), out_shape=jax.ShapeDtyp...  147 us

profile of v4, /device:TPU:0, one launch (start us, length us, event | category | flops | bytes accessed | tf_op | source)
XLA Modules:
  0.0 149.3 jit_solution(9779441932487718998)
XLA Ops:
  0.0 147.1 %shard_map.64 = bf16[64,7168]{1,0:T(8,128)(2,1)} custom-call(bf16[64,7168]{1,0:T(8,128)(2,1)} %tokens.1, s32[4,64]{1,0:T(4,128)} %bitcast.8, bf16[4,64]{1,0:T(4,128)(2,1)} %bitcast.9, bf16[7168,512]{1,0:T(8,128)(2,1)} %bitcast.5, bf16[7168,512]{1,0:T(8,128)(2,1)} %bitcast.6, bf16[512,7168]{1,0:T(8,128)(2,1)} %bitcast.7), custom_call_target="tpu_custom_call" | custom-call | tf_op jit(solution)/shard_map/pallas_call | solution.py:241
  147.1 2.2 %copy.8 = bf16[64,7168]{1,0:T(8,128)(2,1)} copy(bf16[64,7168]{1,0:T(8,128)(2,1)} %shard_map.64) | data formatting | bytes 1835008
